TPU v7x, 32 devices: a whole 2x2x4 slice. The times are simulated.
32 devices in a mesh: lvl: 2 (over core), front: 4 (over z), grid: 4 (over y, x).
Axes of the slice: x: 2, y: 2, z: 4, core: 2. Of those that a mesh axis runs over, the one named last changes fastest.
Arguments:
- child_panel: bfloat16 [4, 2, 4, 2, 128, 512], P('front', None, 'grid', 'lvl'), may hold values from -0.6 to 0.6
- child_blocks: int32 [4], P('front'), may hold values from 6 to 8, as said below
- tile_rows: int32 [2, 4, 4, 64], P('lvl', 'front', 'grid'), may hold values from 0 to 1
- tile_cols: int32 [2, 4, 4, 64], P('lvl', 'front', 'grid'), may hold values from 0 to 7
- tile_parent: int32 [2, 4, 4, 64, 1], P('lvl', 'front', 'grid'), may hold values from 0 to 3; in each aligned block of 64 rows (0 to 63, 64 to 127, ..., all dimensions but the last counted through in order) at most 32 rows name the same one
- tile_place: int32 [2, 4, 4, 64], P('lvl', 'front', 'grid'), may hold values from 0 to 15
- parent_owner: int32 [4], replicated, may hold values from 0 to 3, each once
- parent_front: float32 [4, 2, 4, 2, 128, 2048], P('front', None, 'grid', 'lvl'), may hold values from -1.5 to 151.5, as said below
Outputs:
- factored: float32 [4, 2, 4, 2, 128, 2048], P('front', None, 'grid', 'lvl')
Inputs may be any that keep to these rules, and one draw needn't show every extreme that they name: `child_blocks`: some child front has exactly 8 blocks. `tile_parent`: among the 64 tiles of one device at most 32 name the same parent front, and some parent front is named by exactly 32. `parent_owner`: each front index holds exactly one parent. `parent_front`: the diagonal of each parent's first diagonal block lies between 148.5 and 151.5; all other entries lie within -1.5 to 1.5.
All inputs are finite; a program needn't handle non-finite values.
Results may differ from a plain program's by a relative error of at most 0.00053.
Values may be sent and summed in bfloat16 or wider, within the bound.
A program may use at most 64 MiB of HBM per device.

v0:
```python
import jax
import jax.numpy as jnp
from jax import lax
from jax.sharding import PartitionSpec as P

BLOCK = 256


def broadcast(block, axis, source):
    block = jnp.where(lax.axis_index(axis) == source, block, jnp.zeros_like(block))
    return lax.psum(block, axis)


def per_device(
    child_panel,
    child_blocks,
    tile_rows,
    tile_cols,
    tile_parent,
    tile_place,
    parent_owner,
    parent_front,
):
    level_count = lax.axis_size("lvl")
    grid_count = lax.axis_size("grid")
    front_count = lax.axis_size("front")
    grid_index = lax.axis_index("grid")
    child_local = child_panel.shape[1]
    half_rows = child_panel.shape[4]
    panel_width = child_panel.shape[5]
    parent_local = parent_front.shape[1]
    front_width = parent_front.shape[5]
    block_count = front_width // BLOCK
    slot_count = tile_rows.shape[3]
    capacity = 2 * slot_count // front_count
    slot_total = front_count * capacity
    own_rows = child_panel.reshape(child_local, half_rows, panel_width)
    gathered = lax.all_gather(
        own_rows.reshape(1, child_local, half_rows, panel_width),
        ("lvl", "grid"),
        axis=0,
        tiled=True,
    )
    panel_view = gathered.reshape(level_count, grid_count, child_local, half_rows, panel_width)
    row_local = tile_rows.reshape(slot_count)
    col_block = tile_cols.reshape(slot_count)
    col_grid = col_block % grid_count
    col_local = col_block // grid_count

    def tile_group(indices):

        def one_tile(row_pick, grid_pick, local_pick):
            left_rows = own_rows[row_pick]
            right_rows = panel_view[:, grid_pick, local_pick].reshape(BLOCK, panel_width)
            product = jnp.einsum(
                "ik,jk->ij", left_rows, right_rows, preferred_element_type=jnp.float32
            )
            return (-product).astype(jnp.bfloat16)

        return jax.vmap(one_tile)(indices[0], indices[1], indices[2])

    grouped = (
        jnp.stack([row_local, col_grid, col_local])
        .reshape(3, 8, slot_count // 8)
        .transpose(1, 0, 2)
    )
    update_tiles = lax.map(tile_group, grouped).reshape(slot_count, half_rows, BLOCK)
    child_size = child_blocks[0]
    live_tile = (row_local * grid_count + grid_index < child_size) & (col_block < child_size)
    update_tiles = jnp.where(live_tile[:, None, None], update_tiles, jnp.zeros((), jnp.bfloat16))
    parents = tile_parent.reshape(slot_count)
    places = tile_place.reshape(slot_count)
    front_ids = jnp.arange(front_count, dtype=jnp.int32)
    owners = jnp.sum(
        jnp.where(parents[:, None] == front_ids[None, :], parent_owner[None, :], 0), axis=1
    )
    one_hot = (owners[:, None] == front_ids[None, :]).astype(jnp.int32)
    rank_within = jnp.sum((jnp.cumsum(one_hot, axis=0) - 1) * one_hot, axis=1)
    slot_index = owners * capacity + rank_within
    matches = slot_index[None, :] == jnp.arange(slot_total, dtype=jnp.int32)[:, None]
    filled = jnp.any(matches, axis=1)
    source = jnp.sum(
        jnp.where(matches, jnp.arange(slot_count, dtype=jnp.int32)[None, :], 0), axis=1
    )
    outgoing = jnp.where(filled[:, None, None], update_tiles[source], jnp.zeros((), jnp.bfloat16))
    positions = jnp.where(filled, places[source], -1)
    incoming, landed = (
        lax.all_to_all(outgoing, "front", split_axis=0, concat_axis=0, tiled=True),
        lax.all_to_all(positions, "front", split_axis=0, concat_axis=0, tiled=True),
    )
    spots = parent_local * block_count
    selector = (landed[:, None] == jnp.arange(spots, dtype=jnp.int32)[None, :]).astype(jnp.bfloat16)
    contrib = jnp.einsum("sk,sij->kij", selector, incoming, preferred_element_type=jnp.float32)
    contrib = (
        contrib.reshape(parent_local, block_count, half_rows, BLOCK)
        .transpose(0, 2, 1, 3)
        .reshape(parent_local, half_rows, front_width)
    )
    assembled = parent_front.reshape(parent_local, half_rows, front_width) + contrib
    own_half = assembled[0, :, :BLOCK]
    joined = lax.all_gather(own_half, "lvl", axis=0, tiled=True)
    pivot_block = broadcast(joined, "grid", 0)
    pivot_block = 0.5 * (pivot_block + pivot_block.T)
    lower_factor = jnp.linalg.cholesky(pivot_block)
    first_column = assembled[:, :, :BLOCK].reshape(parent_local * half_rows, BLOCK)
    panel_rows = lax.linalg.triangular_solve(
        lower_factor, first_column, left_side=False, lower=True, transpose_a=True
    )
    panel_rows = panel_rows.reshape(parent_local, half_rows, BLOCK)
    shared = lax.all_gather(
        panel_rows.reshape(1, parent_local, half_rows, BLOCK), ("lvl", "grid"), axis=0, tiled=True
    )
    shared = shared.reshape(level_count, grid_count, parent_local, half_rows, BLOCK)
    schur = jnp.einsum("rik,lgsjk->risglj", panel_rows, shared, precision=lax.Precision.HIGHEST)
    schur = schur.reshape(parent_local, half_rows, front_width)
    trailing = assembled[:, :, BLOCK:] - schur[:, :, BLOCK:]
    result = jnp.concatenate([panel_rows, trailing], axis=2)
    return result.reshape(1, parent_local, 1, 1, half_rows, front_width)


def solution(mesh):
    return jax.shard_map(
        per_device,
        mesh=mesh,
        in_specs=(
            P("front", None, "grid", "lvl", None, None),
            P("front"),
            P("lvl", "front", "grid", None),
            P("lvl", "front", "grid", None),
            P("lvl", "front", "grid", None, None),
            P("lvl", "front", "grid", None),
            P(),
            P("front", None, "grid", "lvl", None, None),
        ),
        out_specs=P("front", None, "grid", "lvl", None, None),
        check_vma=False,
    )
```

profile of v0, /device:TPU:0, one launch (start us, length us, event | category | flops | bytes accessed | tf_op | source)
XLA Modules:
  0.0 450.2 jit_solution(15282769628164825725)
XLA Ops:
  7.3 0.8 select_reduce_fusion.4
  8.6 1.2 gather_fusion.2
  10.6 6.3 %all-to-all-start = ((s32[4,32,1]{1,2,0:T(1,128)}), s32[4,32,1]{1,2,0:T(1,128)S(1)}, u32[]{:S(2)}, u32[]{:S(2)}) async-start(s32[4,32,1]{1,2,0:T(1,128)} %bitcast.12), calls=%async_computation | async-start | bytes 4096 | tf_op jit(solution)/shard_map/all_to_all | solution.py:89
  17.5 1.3 reduce.21
  18.8 1.3 reduce.22
  21.6 18.3 %all-gather.7.cloned.1.call-done = bf16[8,2,1,1,128,512]{5,4,3,2,1,0:T(8,128)(2,1)} async-done(((bf16[1,2,1,1,128,512]{5,4,3,2,1,0:T(8,128)(2,1)}), bf16[8,2,1,1,128,512]{5,4,3,2,1,0:T(8,128)(2,1)}) %all-gather.7.cloned.1.call-update) | async-done | bytes 2097168 | tf_op jit(solution)/shard_map/all_gather | solution.py:38
  39.9 3.1 copy.49
  43.0 36.4 %while.11 = (s32[]{:T(128)}, bf16[8,8,128,256]{3,2,1,0:T(8,128)(2,1)}, s32[8,3,8]{2,0,1:T(8,128)S(1)}, bf16[2,128,512]{2,1,0:T(8,128)(2,1)S(1)}, bf16[2,4,2,128,...) while((s32[]{:T(128)}, bf16[8,8,128,256]{3,2,1,0:T(8,128)(2,1)}, s32[8,3,8]{2,0,1:T(8,128)S(1)}, ...), condition=%wide.region_6.7_spmd, body=%wide.region_5.6_spmd.sunk | while | flops 268959872 | bytes 9962529 | solution.py:67
  43.1 2.3 gather_fusion.1
  46.0 1.6 fusion.43
  47.6 2.3 gather_fusion.1
  50.5 1.6 fusion.43
  52.1 2.3 gather_fusion.1
  55.1 1.6 fusion.43
  56.7 2.3 gather_fusion.1
  59.6 1.6 fusion.43
  61.3 2.3 gather_fusion.1
  64.2 1.6 fusion.43
  65.8 2.3 gather_fusion.1
  68.7 1.6 fusion.43
  70.4 2.3 gather_fusion.1
  73.3 1.6 fusion.43
  74.9 2.3 gather_fusion.1
  77.8 1.6 fusion.43
  79.4 4.5 bitcast_select_fusion
  83.9 8.7 %gather_fusion.3 = bf16[128,128,256]{2,1,0:T(8,128)(2,1)} fusion(bf16[64,128,256]{2,1,0:T(8,128)(2,1)} %bitcast_select_fusion, s32[1024]{0:T(1024)S(1)} %pad_clamp_fusion), kind=kCustom, calls=%fused_computation.3 | custom fusion | bytes 16777728 | tf_op jit(solution)/shard_map/gather | solution.py:85
  92.6 7.2 %broadcast_select_fusion = bf16[128,128,256]{2,1,0:T(8,128)(2,1)} fusion(bf16[128,128,256]{2,1,0:T(8,128)(2,1)} %gather_fusion.3, pred[128]{0:T(512)(128)(4,1)S(1)} %fusion.20), kind=kLoop, calls=%fused_computation.23 | loop fusion | flops 4194304 | bytes 16777344 | tf_op jit(solution)/shard_map/jit(_where)/select_n | solution.py:85
  99.8 5.8 %all-to-all-start.1 = ((bf16[128,128,256]{2,1,0:T(8,128)(2,1)}), bf16[128,128,256]{2,1,0:T(8,128)(2,1)}, u32[]{:S(2)}, u32[]{:S(2)}) async-start(bf16[128,128,256]{2,1,0:T(8,128)(2,1)} %broadcast_select_fusion), calls=%async_computation.1 | async-start | bytes 16777216 | tf_op jit(solution)/shard_map/all_to_all | solution.py:88
  105.7 1.9 copy.46
  108.3 181.1 %all-to-all-done.1 = bf16[128,128,256]{2,1,0:T(8,128)(2,1)} async-done(((bf16[128,128,256]{2,1,0:T(8,128)(2,1)}), bf16[128,128,256]{2,1,0:T(8,128)(2,1)}, u32[]{:S(2)}, u32[]{:S(2)}) %all-to-all-start.1) | async-done | bytes 8388640 | tf_op jit(solution)/shard_map/all_to_all | solution.py:88
  289.4 7.9 %fusion.8 = f32[2,8,128,256]{3,1,0,2:T(8,128)S(1)} fusion(bf16[128,128,256]{2,1,0:T(8,128)(2,1)} %all-to-all-done.1, s32[128]{0:T(128)S(1)} %eq.71), kind=kOutput, calls=%fused_computation.28 | convolution fusion | flops 134219776 | bytes 10486272 | tf_op jit(solution)/shard_map/sk,sij->kij/dot_general | solution.py:93
  297.3 1.9 copy.51
  299.2 2.4 bitcast_add_fusion
  301.6 2.0 all-gather.1
  304.8 40.8 %all-reduce.4.cloned.1.call-done = f32[256,256]{0,1:T(8,128)} async-done(((f32[256,256]{0,1:T(8,128)}), f32[256,256]{0,1:T(8,128)}) %all-reduce.4.cloned.1.call-update) | async-done | bytes 262160 | tf_op jit(solution)/shard_map/psum | solution.py:11
  345.6 1.1 copy.53
  346.7 1.0 fusion.12
  347.9 11.7 %cholesky.49 = f32[128,128]{1,0:T(8,128)S(1)} custom-call(f32[128,128]{1,0:T(8,128)S(1)} %cholesky.115), custom_call_target="Cholesky" | custom-call | tf_op jit(solution)/shard_map/jit(cholesky)/cholesky | solution.py:104
  359.7 9.8 %custom-call.14 = f32[1,128,128]{1,2,0:T(8,128)S(1)} custom-call(f32[1,128,128]{2,1,0:T(8,128)S(1)} %get-tuple-element.86), custom_call_target="InvertDiagBlocksLowerTriangular" | custom-call | tf_op jit(solution)/shard_map/jit(cholesky)/cholesky | solution.py:104
  370.0 11.7 %cholesky.103 = f32[128,128]{1,0:T(8,128)S(1)} custom-call(f32[128,128]{1,0:T(8,128)S(1)} %convolution_subtract_fusion.1), custom_call_target="Cholesky" | custom-call | tf_op jit(solution)/shard_map/jit(cholesky)/cholesky | solution.py:104
  383.9 4.3 while.12
  384.7 1.4 bitcast_dynamic-update-slice_fusion.2
  386.7 1.4 bitcast_dynamic-update-slice_fusion.2
  388.2 19.7 %custom-call.15 = f32[2,128,128]{1,2,0:T(8,128)S(1)} custom-call(f32[2,128,128]{2,1,0:T(8,128)S(1)} %get-tuple-element.40), custom_call_target="InvertDiagBlocksLowerTriangular" | custom-call | tf_op jit(solution)/shard_map/triangular_solve | solution.py:106
  409.8 1.1 copy.58
  410.9 27.0 %all-gather.5.cloned.1.call-done = f32[8,2,128,256]{3,2,1,0:T(8,128)} async-done(((f32[1,2,128,256]{3,2,1,0:T(8,128)}), f32[8,2,128,256]{3,2,1,0:T(8,128)}) %all-gather.5.cloned.1.call-update) | async-done | bytes 2097168 | tf_op jit(solution)/shard_map/all_gather | solution.py:110
  437.8 3.4 convolution_bitcast_fusion
  441.8 1.8 copy.59
  (79 shorter events, 15.5 us)
Async XLA Ops:
  6.5 2.1 copy-start
  6.5 33.4 %all-gather.7.cloned.1.call-start = ((), (), s32[]{:S(2)}) async-start(), calls=%async_computation.4 | async-start | bytes 2359296 | tf_op jit(solution)/shard_map/all_gather | solution.py:38
  10.6 89.2 %all-to-all-start = ((s32[4,32,1]{1,2,0:T(1,128)}), s32[4,32,1]{1,2,0:T(1,128)S(1)}, u32[]{:S(2)}, u32[]{:S(2)}) async-start(s32[4,32,1]{1,2,0:T(1,128)} %bitcast.12), calls=%async_computation | async-start | bytes 4096 | tf_op jit(solution)/shard_map/all_to_all | solution.py:89
  39.9 3.1 copy-start.2
  99.8 5.9 %copy-start.3 = (f32[1,2,1,1,128,2048]{5,4,3,2,1,0:T(8,128)S(1)}, f32[1,2,1,1,128,2048]{5,4,3,2,1,0:T(8,128)}, u32[]{:S(2)}) copy-start(f32[1,2,1,1,128,2048]{5,4,3,2,1,0:T(8,128)} %param.17) | copy-start | bytes 6291460
  99.8 189.6 %all-to-all-start.1 = ((bf16[128,128,256]{2,1,0:T(8,128)(2,1)}), bf16[128,128,256]{2,1,0:T(8,128)(2,1)}, u32[]{:S(2)}, u32[]{:S(2)}) async-start(bf16[128,128,256]{2,1,0:T(8,128)(2,1)} %broadcast_select_fusion), calls=%async_computation.1 | async-start | bytes 16777216 | tf_op jit(solution)/shard_map/all_to_all | solution.py:88
  105.6 240.0 %all-reduce.4.cloned.1.call-start = ((), (), s32[]{:S(2)}) async-start(), calls=%async_computation.2 | async-start | bytes 524288 | tf_op jit(solution)/shard_map/psum | solution.py:11
  304.4 133.4 %all-gather.5.cloned.1.call-start = ((), (), s32[]{:S(2)}) async-start(), calls=%async_computation.3 | async-start | bytes 2359296 | tf_op jit(solution)/shard_map/all_gather | solution.py:110
  441.7 2.0 copy-start.1
Sparse Core Ops, SparseCore 0:
  9.2 30.6 all-gather.6
  304.5 41.0 all-reduce.3
  409.9 27.8 all-gather.4
where the time goes:
time: 451 us; the launch traced here: 450 us
  waiting for transfers between devices  268 us (59%)
  other arithmetic  75.5 us (17%)
  local copies, waits for them, and re-layouts  50.8 us (11%)
  matrix products  25.8 us (6%)
  between operations  15.4 us (3%)
  starting transfers between devices  12.4 us (3%)
    all_to_all x1, waiting for transfers between devices, per_device(): lax.all_to_all(outgoing, 'front', split_axis=0, concat_axis=0, tiled=True)  181 us
    psum x1, waiting for transfers between devices, broadcast(): return lax.psum(block, axis)  40.8 us
    another operation x6, other arithmetic, per_device(): lower_factor = jnp.linalg.cholesky(pivot_block)  34 us
    all_gather x1, waiting for transfers between devices, per_device(): lax.all_gather(panel_rows.reshape(1, parent_local, half_rows, BLOCK), ('l...  27 us
    another operation x4, other arithmetic, per_device(): lax.linalg.triangular_solve(lower_factor, first_column, left_side=False,...  19.7 us
    all_gather x1, waiting for transfers between devices, per_device(): lax.all_gather(own_rows.reshape(1, child_local, half_rows, panel_width),...  18.3 us
    gather x8, local copies, waits for them, and re-layouts, one_tile(): panel_view[:, grid_pick, local_pick].reshape(BLOCK, panel_width)  18.2 us
    dot_general x8, matrix products, one_tile(): jnp.einsum('ik,jk->ij', left_rows, right_rows, preferred_element_type=jnp...  13 us
  transfers between devices with their start and end apart: 5, of which 4 were waited for; matrix products, arithmetic and copies ran while one was open for 16% of the time, Pallas kernels for 0%

commit v1 on v0

--- a/solution.py
+++ b/solution.py
@@ -8,7 +8,8 @@
 
 def broadcast(block, axis, source):
     block = jnp.where(lax.axis_index(axis) == source, block, jnp.zeros_like(block))
-    return lax.psum(block, axis)
+    build_views = lambda lane_axis, load: lax.all_gather(load, lane_axis).sum(axis=0)
+    return build_views(axis, block)
 
 
 def per_device(

time: 451 us -> 441 us (0.978)
  waiting for transfers between devices: 268 us -> 254 us
    psum x1 -> x0, waiting for transfers between devices: 40.8 us -> none  [broadcast(): return lax.psum(block, axis)]
    all_gather x0 -> x1, waiting for transfers between devices: none -> 24.6 us  [broadcast(): lax.all_gather(load, lane_axis).sum(axis=0)]
  transfers between devices with their start and end apart: 5 -> 5, of which waited for: 4 -> 4; matrix products, arithmetic and copies ran while one was open for 16% -> 15% of each run, Pallas kernels for 0% -> 0%
where the time goes in v1:
time: 441 us; the launch traced here: 440 us
  waiting for transfers between devices  254 us (58%)
  other arithmetic  79.9 us (18%)
  local copies, waits for them, and re-layouts  49.7 us (11%)
  matrix products  25.8 us (6%)
  between operations  15.4 us (3%)
  starting transfers between devices  12.2 us (3%)
    all_to_all x1, waiting for transfers between devices, per_device(): lax.all_to_all(outgoing, 'front', split_axis=0, concat_axis=0, tiled=True)  183 us
    another operation x6, other arithmetic, per_device(): lower_factor = jnp.linalg.cholesky(pivot_block)  34 us
    all_gather x1, waiting for transfers between devices, per_device(): lax.all_gather(panel_rows.reshape(1, parent_local, half_rows, BLOCK), ('l...  27.7 us
    all_gather x1, waiting for transfers between devices, broadcast(): lax.all_gather(load, lane_axis).sum(axis=0)  24.6 us
    another operation x4, other arithmetic, per_device(): lax.linalg.triangular_solve(lower_factor, first_column, left_side=False,...  19.7 us
    all_gather x1, waiting for transfers between devices, per_device(): lax.all_gather(own_rows.reshape(1, child_local, half_rows, panel_width),...  18.3 us
    gather x8, local copies, waits for them, and re-layouts, one_tile(): panel_view[:, grid_pick, local_pick].reshape(BLOCK, panel_width)  18.2 us
    dot_general x8, matrix products, one_tile(): jnp.einsum('ik,jk->ij', left_rows, right_rows, preferred_element_type=jnp...  13 us
  transfers between devices with their start and end apart: 5, of which 4 were waited for; matrix products, arithmetic and copies ran while one was open for 15% of the time, Pallas kernels for 0%

profile of v1, /device:TPU:0, one launch (start us, length us, event | category | flops | bytes accessed | tf_op | source)
XLA Modules:
  0.0 439.8 jit_solution(12493500229311847285)
XLA Ops:
  7.3 0.8 select_reduce_fusion.4
  8.6 1.2 gather_fusion.2
  10.6 6.3 %all-to-all-start = ((s32[4,32,1]{1,2,0:T(1,128)}), s32[4,32,1]{1,2,0:T(1,128)S(1)}, u32[]{:S(2)}, u32[]{:S(2)}) async-start(s32[4,32,1]{1,2,0:T(1,128)} %bitcast.12), calls=%async_computation | async-start | bytes 4096 | tf_op jit(solution)/shard_map/all_to_all | solution.py:90
  17.5 1.3 reduce.21
  18.9 1.3 reduce.22
  21.6 18.3 %all-gather.10.cloned.1.call-done = bf16[8,2,1,1,128,512]{5,4,3,2,1,0:T(8,128)(2,1)} async-done(((bf16[1,2,1,1,128,512]{5,4,3,2,1,0:T(8,128)(2,1)}), bf16[8,2,1,1,128,512]{5,4,3,2,1,0:T(8,128)(2,1)}) %all-gather.10.cloned.1.call-update) | async-done | bytes 2097168 | tf_op jit(solution)/shard_map/all_gather | solution.py:39
  39.9 3.1 copy.53
  43.0 36.4 %while.11 = (s32[]{:T(128)}, bf16[8,8,128,256]{3,2,1,0:T(8,128)(2,1)}, s32[8,3,8]{2,0,1:T(8,128)S(1)}, bf16[2,128,512]{2,1,0:T(8,128)(2,1)S(1)}, bf16[2,4,2,128,...) while((s32[]{:T(128)}, bf16[8,8,128,256]{3,2,1,0:T(8,128)(2,1)}, s32[8,3,8]{2,0,1:T(8,128)S(1)}, ...), condition=%wide.region_6.7_spmd, body=%wide.region_5.6_spmd.sunk | while | flops 268959872 | bytes 9962529 | solution.py:68
  43.0 2.3 gather_fusion.1
  45.9 1.6 fusion.43
  47.6 2.3 gather_fusion.1
  50.5 1.6 fusion.43
  52.1 2.3 gather_fusion.1
  55.0 1.6 fusion.43
  56.7 2.3 gather_fusion.1
  59.6 1.6 fusion.43
  61.2 2.3 gather_fusion.1
  64.1 1.6 fusion.43
  65.8 2.3 gather_fusion.1
  68.7 1.6 fusion.43
  70.3 2.3 gather_fusion.1
  73.3 1.6 fusion.43
  74.9 2.3 gather_fusion.1
  77.8 1.6 fusion.43
  79.4 4.5 %bitcast_select_fusion = bf16[64,128,256]{2,1,0:T(8,128)(2,1)} fusion(bf16[8,8,128,256]{3,2,1,0:T(8,128)(2,1)} %get-tuple-element.32, pred[64]{0:T(512)(128)(4,1)S(1)} %and_bitcast_fusion), kind=kLoop, calls=%fused_computation.24 | loop fusion | flops 2097152 | bytes 8388672 | tf_op jit(solution)/shard_map/jit(_where)/select_n | solution.py:71
  83.9 8.7 %gather_fusion.3 = bf16[128,128,256]{2,1,0:T(8,128)(2,1)} fusion(bf16[64,128,256]{2,1,0:T(8,128)(2,1)} %bitcast_select_fusion, s32[1024]{0:T(1024)S(1)} %pad_clamp_fusion), kind=kCustom, calls=%fused_computation.3 | custom fusion | bytes 16777728 | tf_op jit(solution)/shard_map/gather | solution.py:86
  92.6 7.2 %broadcast_select_fusion = bf16[128,128,256]{2,1,0:T(8,128)(2,1)} fusion(bf16[128,128,256]{2,1,0:T(8,128)(2,1)} %gather_fusion.3, pred[128]{0:T(512)(128)(4,1)S(1)} %fusion.21), kind=kLoop, calls=%fused_computation.23 | loop fusion | flops 4194304 | bytes 16777344 | tf_op jit(solution)/shard_map/jit(_where)/select_n | solution.py:86
  99.8 5.7 %all-to-all-start.1 = ((bf16[128,128,256]{2,1,0:T(8,128)(2,1)}), bf16[128,128,256]{2,1,0:T(8,128)(2,1)}, u32[]{:S(2)}, u32[]{:S(2)}) async-start(bf16[128,128,256]{2,1,0:T(8,128)(2,1)} %broadcast_select_fusion), calls=%async_computation.1 | async-start | bytes 16777216 | tf_op jit(solution)/shard_map/all_to_all | solution.py:89
  106.2 183.0 %all-to-all-done.1 = bf16[128,128,256]{2,1,0:T(8,128)(2,1)} async-done(((bf16[128,128,256]{2,1,0:T(8,128)(2,1)}), bf16[128,128,256]{2,1,0:T(8,128)(2,1)}, u32[]{:S(2)}, u32[]{:S(2)}) %all-to-all-start.1) | async-done | bytes 8388640 | tf_op jit(solution)/shard_map/all_to_all | solution.py:89
  289.3 7.9 %fusion.8 = f32[2,128,8,256]{3,2,0,1:T(8,128)S(1)} fusion(bf16[128,128,256]{2,1,0:T(8,128)(2,1)} %all-to-all-done.1, s32[128]{0:T(128)S(1)} %eq.71), kind=kOutput, calls=%fused_computation.28 | convolution fusion | flops 134219776 | bytes 10486272 | tf_op jit(solution)/shard_map/sk,sij->kij/dot_general | solution.py:94
  297.2 2.3 reshape.400
  299.5 3.5 copy_add_fusion
  303.0 2.0 all-gather.1
  306.0 24.6 %all-gather.12.cloned.1.call-done = f32[1,1024,256]{2,1,0:T(8,128)} async-done(((f32[1,256,256]{2,1,0:T(8,128)}), f32[1,1024,256]{2,1,0:T(8,128)}) %all-gather.12.cloned.1.call-update) | async-done | bytes 1048592 | tf_op jit(solution)/shard_map/all_gather | solution.py:11
  330.7 1.3 reduce_sum.42
  332.2 11.7 %cholesky.49 = f32[128,128]{1,0:T(8,128)S(1)} custom-call(f32[128,128]{1,0:T(8,128)S(1)} %cholesky.115), custom_call_target="Cholesky" | custom-call | tf_op jit(solution)/shard_map/jit(cholesky)/cholesky | solution.py:105
  344.0 9.8 %custom-call.14 = f32[1,128,128]{1,2,0:T(8,128)S(1)} custom-call(f32[1,128,128]{2,1,0:T(8,128)S(1)} %get-tuple-element.91), custom_call_target="InvertDiagBlocksLowerTriangular" | custom-call | tf_op jit(solution)/shard_map/jit(cholesky)/cholesky | solution.py:105
  354.3 11.7 %cholesky.103 = f32[128,128]{1,0:T(8,128)S(1)} custom-call(f32[128,128]{1,0:T(8,128)S(1)} %convolution_subtract_fusion.1), custom_call_target="Cholesky" | custom-call | tf_op jit(solution)/shard_map/jit(cholesky)/cholesky | solution.py:105
  368.2 4.3 while.12
  369.0 1.4 bitcast_dynamic-update-slice_fusion.2
  371.0 1.4 bitcast_dynamic-update-slice_fusion.2
  372.5 19.7 %custom-call.15 = f32[2,128,128]{1,2,0:T(8,128)S(1)} custom-call(f32[2,128,128]{2,1,0:T(8,128)S(1)} %get-tuple-element.40), custom_call_target="InvertDiagBlocksLowerTriangular" | custom-call | tf_op jit(solution)/shard_map/triangular_solve | solution.py:107
  394.4 27.7 %all-gather.8.cloned.1.call-done = f32[8,2,128,256]{3,2,1,0:T(8,128)} async-done(((f32[1,2,128,256]{3,2,1,0:T(8,128)}), f32[8,2,128,256]{3,2,1,0:T(8,128)}) %all-gather.8.cloned.1.call-update) | async-done | bytes 2097168 | tf_op jit(solution)/shard_map/all_gather | solution.py:111
  422.1 3.4 convolution_bitcast_fusion
  425.7 1.4 slice.98
  427.1 2.8 copy.70
  429.9 1.8 slice_subtract_fusion
  431.7 1.6 maximum_bitcast_fusion
  (76 shorter events, 15.3 us)
Async XLA Ops:
  6.5 2.1 copy-start
  6.5 33.3 %all-gather.10.cloned.1.call-start = ((), (), s32[]{:S(2)}) async-start(), calls=%async_computation.3 | async-start | bytes 2359296 | tf_op jit(solution)/shard_map/all_gather | solution.py:39
  10.6 89.2 %all-to-all-start = ((s32[4,32,1]{1,2,0:T(1,128)}), s32[4,32,1]{1,2,0:T(1,128)S(1)}, u32[]{:S(2)}, u32[]{:S(2)}) async-start(s32[4,32,1]{1,2,0:T(1,128)} %bitcast.12), calls=%async_computation | async-start | bytes 4096 | tf_op jit(solution)/shard_map/all_to_all | solution.py:90
  39.9 3.1 copy-start.2
  99.8 189.5 %all-to-all-start.1 = ((bf16[128,128,256]{2,1,0:T(8,128)(2,1)}), bf16[128,128,256]{2,1,0:T(8,128)(2,1)}, u32[]{:S(2)}, u32[]{:S(2)}) async-start(bf16[128,128,256]{2,1,0:T(8,128)(2,1)} %broadcast_select_fusion), calls=%async_computation.1 | async-start | bytes 16777216 | tf_op jit(solution)/shard_map/all_to_all | solution.py:89
  105.5 225.2 %all-gather.12.cloned.1.call-start = ((), (), s32[]{:S(2)}) async-start(), calls=%async_computation.4 | async-start | bytes 1310720 | tf_op jit(solution)/shard_map/all_gather | solution.py:11
  305.7 116.4 %all-gather.8.cloned.1.call-start = ((), (), s32[]{:S(2)}) async-start(), calls=%async_computation.2 | async-start | bytes 2359296 | tf_op jit(solution)/shard_map/all_gather | solution.py:111
  429.8 3.4 copy-start.1
Sparse Core Ops, SparseCore 0:
  9.2 30.5 all-gather.9
  305.9 24.7 all-gather.11
  394.2 27.8 all-gather.7
